TPU v7x, 32 devices: a whole 2x2x4 slice. The times are simulated.
32 devices in a mesh: head: 4 (over y, core), st: 8 (over z, x).
Axes of the slice: x: 2, y: 2, z: 4, core: 2. Of those that a mesh axis runs over, the one named last changes fastest.
Arguments:
- queries: bfloat16 [8, 1024, 40, 128], P('st', 'head'), may hold values from -68 to 68
- key_vectors: bfloat16 [8, 1024, 40, 128], P('st', 'head'), may hold values from -14 to 14
- value_vectors: bfloat16 [8, 1024, 40, 128], P('st', 'head'), may hold values from -4.5 to 4.5
- block_lists: int32 [64, 40, 8], P('st', 'head'), may hold values from -1 to 7, as said below
Outputs:
- attended: bfloat16 [8, 1024, 40, 128], P('st', 'head')
Inputs may be any that keep to these rules, and one draw needn't show every extreme that they name: `block_lists`: for each query tile and head: the selected key blocks of its own tube in ascending order, each once, then -1 in the remaining entries; the tile's own block (block t for tile t) is always selected; at most 8 blocks, and in every draw some tile selects all 8 blocks in every head.
All inputs are finite; a program needn't handle non-finite values.
Results may differ from a plain program's by a relative error of at most 0.0043.
Values may be sent and summed in bfloat16 or wider, within the bound.
No kernel may reach another device: no remote copies, remote signals or barrier semaphores. Data moves between devices by JAX's collectives and lax.ppermute only.
A program may use at most 128 MiB of HBM per device.

v0:
```python
import jax
import jax.numpy as jnp
from jax import lax
from jax.sharding import PartitionSpec as P

BLK = 128


def attend_dense(query_rows, key_rows, value_rows, chosen):
    tile_count, head_count, slots = chosen.shape
    head_width = query_rows.shape[-1]
    blocks = key_rows.shape[0] // BLK
    query_tiles = query_rows.reshape(tile_count, BLK, head_count, head_width)
    key_blocks = key_rows.reshape(blocks, BLK, head_count, head_width)
    value_blocks = value_rows.reshape(blocks, BLK, head_count, head_width)
    block_pos = jnp.arange(blocks, dtype=jnp.int32)
    picked = jnp.any(chosen[:, :, :, None] == block_pos[None, None, None, :], axis=2)
    scores = jnp.einsum(
        "tqhd,bkhd->htqbk", query_tiles, key_blocks, preferred_element_type=jnp.float32
    ) * head_width ** (-0.5)
    allowed = jnp.transpose(picked, (1, 0, 2))[:, :, None, :, None]
    scores = jnp.where(allowed, scores, -jnp.inf)
    row_max = jnp.max(scores, axis=(3, 4), keepdims=True)
    weights = jnp.exp(scores - row_max)
    row_total = jnp.sum(weights, axis=(3, 4))
    summed = jnp.einsum(
        "htqbk,bkhd->tqhd",
        weights.astype(jnp.bfloat16),
        value_blocks,
        preferred_element_type=jnp.float32,
    )
    result = summed / jnp.transpose(row_total, (1, 2, 0))[..., None]
    return result.reshape(tile_count * BLK, head_count, head_width).astype(jnp.bfloat16)


def attend(query_rows, key_rows, value_rows, chosen):
    return attend_dense(query_rows, key_rows, value_rows, chosen)


def body(queries, key_vectors, value_vectors, block_lists):
    head_devs = lax.axis_size("head")
    st_devs = lax.axis_size("st")
    local_frames, local_space, all_heads, head_width = queries.shape
    group_width = all_heads // head_devs
    tubes_here = st_devs // head_devs
    sub_width = local_space // tubes_here

    def to_column(source):
        shaped = source.reshape(
            local_frames, tubes_here, sub_width, head_devs, group_width, head_width
        )
        shaped = jnp.transpose(shaped, (1, 3, 0, 2, 4, 5))
        return shaped.reshape(st_devs, local_frames, sub_width, group_width, head_width)

    tube_query, tube_key, tube_value = (
        lax.all_to_all(to_column(queries), "st", split_axis=0, concat_axis=0, tiled=True),
        lax.all_to_all(to_column(key_vectors), "st", split_axis=0, concat_axis=0, tiled=True),
        lax.all_to_all(to_column(value_vectors), "st", split_axis=0, concat_axis=0, tiled=True),
    )
    lists_heads = lax.all_gather(block_lists, "head", axis=1, tiled=True)
    lists_all = lax.all_gather(lists_heads, "st", axis=0, tiled=True)
    tube_rows = block_lists.shape[0]
    tube_here = lax.axis_index("head") * tubes_here + lax.axis_index("st") // head_devs
    group_here = lax.axis_index("st") % head_devs
    lists_here = lax.dynamic_slice(
        lists_all,
        (tube_here * tube_rows, group_here * group_width, jnp.int32(0)),
        (tube_rows, group_width, block_lists.shape[2]),
    )
    row_count = tube_query.size // (group_width * head_width)
    query_rows = tube_query.reshape(row_count, group_width, head_width)
    key_rows = tube_key.reshape(row_count, group_width, head_width)
    value_rows = tube_value.reshape(row_count, group_width, head_width)
    result_rows = attend(query_rows, key_rows, value_rows, lists_here)
    result = result_rows.reshape(st_devs, local_frames, sub_width, group_width, head_width)
    spread = lax.all_to_all(result, "st", split_axis=0, concat_axis=0, tiled=True)
    spread = spread.reshape(tubes_here, head_devs, local_frames, sub_width, group_width, head_width)
    spread = jnp.transpose(spread, (2, 0, 3, 1, 4, 5))
    attended = spread.reshape(local_frames, local_space, all_heads, head_width)
    return attended


def solution(mesh):
    in_specs = (
        P("st", "head", None, None),
        P("st", "head", None, None),
        P("st", "head", None, None),
        P("st", "head", None),
    )
    out_specs = P("st", "head", None, None)
    return jax.shard_map(body, mesh=mesh, in_specs=in_specs, out_specs=out_specs, check_vma=False)
```

profile of v0, /device:TPU:0, one launch (start us, length us, event | category | flops | bytes accessed | tf_op | source)
XLA Modules:
  0.0 300.3 jit_solution(10547766003020081770)
XLA Ops:
  0.0 2.4 copy.52
  2.4 1.8 copy.53
  4.2 7.3 %all-to-all-start = ((bf16[8,1,128,10,128]{4,2,3,1,0:T(8,128)(2,1)}), bf16[8,1,128,10,128]{4,2,3,1,0:T(8,128)(2,1)S(1)}, u32[]{:S(2)}, u32[]{:S(2)}) async-start(bf16[8,1,128,10,128]{4,2,3,1,0:T(8,128)(2,1)} %bitcast.55), calls=%async_computation | async-start | bytes 5242880 | tf_op jit(solution)/shard_map/all_to_all | solution.py:56
  11.5 2.4 copy.55
  13.8 0.0 copy-start
  13.9 1.8 copy.56
  15.7 55.3 %all-to-all-done = bf16[8,1,128,10,128]{4,2,3,1,0:T(8,128)(2,1)S(1)} async-done(((bf16[8,1,128,10,128]{4,2,3,1,0:T(8,128)(2,1)}), bf16[8,1,128,10,128]{4,2,3,1,0:T(8,128)(2,1)S(1)}, u32[]{:S(2)}, u32[]{:S(2)}) %all-to-all-start) | async-done | bytes 2621472 | tf_op jit(solution)/shard_map/all_to_all | solution.py:56
  71.0 4.4 %all-to-all-start.1 = ((bf16[8,1,128,10,128]{4,2,3,1,0:T(8,128)(2,1)}), bf16[8,1,128,10,128]{4,2,3,1,0:T(8,128)(2,1)}, u32[]{:S(2)}, u32[]{:S(2)}) async-start(bf16[8,1,128,10,128]{4,2,3,1,0:T(8,128)(2,1)} %bitcast.53), calls=%async_computation.1 | async-start | bytes 5242880 | tf_op jit(solution)/shard_map/all_to_all | solution.py:57
  75.4 0.0 copy-done
  75.4 0.1 copy.49
  75.5 5.5 %all_gather.6 = s32[8,40,8]{2,0,1:T(8,128)S(1)} all-gather(s32[8,10,8]{2,0,1:T(8,128)S(1)} %copy.49), channel_id=1, replica_groups=mesh['head'=4,'st'=8] {'head'}, dimensions={1}, use_global_device_ids=true | all-gather | bytes 12800 | tf_op jit(solution)/shard_map/all_gather | solution.py:60
  81.0 0.1 copy.50
  81.1 2.4 copy.58
  83.5 1.8 copy.59
  85.3 69.4 %all_gather.7 = s32[64,40,8]{1,2,0:T(8,128)S(1)} all-gather(s32[8,40,8]{1,2,0:T(8,128)S(1)} %copy.50), channel_id=1, replica_groups=mesh['head'=4,'st'=8] {'st'}, dimensions={0}, use_global_device_ids=true | all-gather | bytes 92160 | tf_op jit(solution)/shard_map/all_gather | solution.py:61
  154.7 0.1 constant_dynamic-slice_fusion
  154.8 0.0 all-to-all-done.1
  154.8 4.4 %all-to-all-start.2 = ((bf16[8,1,128,10,128]{4,2,3,1,0:T(8,128)(2,1)}), bf16[8,1,128,10,128]{4,2,3,1,0:T(8,128)(2,1)}, u32[]{:S(2)}, u32[]{:S(2)}) async-start(bf16[8,1,128,10,128]{4,2,3,1,0:T(8,128)(2,1)} %bitcast.54), calls=%async_computation.2 | async-start | bytes 5242880 | tf_op jit(solution)/shard_map/all_to_all | solution.py:58
  159.3 0.1 copy.51
  159.4 16.5 %fusion = (f32[10,8,128]{2,1,0:T(8,128)S(1)}, f32[10,8,128,8,128]{2,4,3,1,0:T(8,128)}) fusion(pred[10,8,8]{2,1,0:T(8,128)(4,1)S(1)} %copy.51, bf16[8,1,128,10,128]{4,2,3,1,0:T(8,128)(2,1)} %all-to-all-done.1, bf16[8,1,128,10,128]{4,2,3,1,0:T(8,128)(2,1)S(1)} %all-to-all-done), kind=kOutput, calls=%fused_computation.2 | convolution fusion | flops 2715801600 | bytes 47227520 | tf_op jit(solution)/shard_map/tqhd,bkhd->htqbk/dot_general | solution.py:18
  175.9 17.9 %fusion.1 = f32[10,8,128]{2,1,0:T(8,128)S(1)} fusion(f32[10,8,128,8,128]{2,4,3,1,0:T(8,128)} %get-tuple-element.6, f32[10,8,128]{2,1,0:T(8,128)S(1)} %get-tuple-element.5, pred[10,8,8]{2,1,0:T(8,128)(4,1)S(1)} %copy.51), kind=kLoop, calls=%fused_computation.3 | loop fusion | flops 41932800 | bytes 42025600 | tf_op jit(solution)/shard_map/reduce_sum | solution.py:25
  193.8 20.4 %all-to-all-done.2 = bf16[8,1,128,10,128]{4,2,3,1,0:T(8,128)(2,1)} async-done(((bf16[8,1,128,10,128]{4,2,3,1,0:T(8,128)(2,1)}), bf16[8,1,128,10,128]{4,2,3,1,0:T(8,128)(2,1)}, u32[]{:S(2)}, u32[]{:S(2)}) %all-to-all-start.2) | async-done | bytes 2621472 | tf_op jit(solution)/shard_map/all_to_all | solution.py:58
  214.1 19.7 %fusion.14 = bf16[8,1,128,10,128]{4,2,0,3,1:T(8,128)(2,1)S(1)} fusion(f32[8,128,10]{1,0,2:T(8,128)S(1)} %bitcast.61, bf16[8,1,128,10,128]{4,2,3,1,0:T(8,128)(2,1)} %all-to-all-done.2, f32[10,8,128,8,128]{2,4,3,1,0:T(8,128)} %get-tuple-element.6, f32[10,8,128]{2,1,0:T(8,128)S(1)} %get-tuple-element.5, pred[10,8,8]{2,1,0:T(8,128)(4,1)S(1)} %copy.51), kind=kOutput, calls=%fused_computation.16 | convolution fusion | flops 2728919040 | bytes 47268480 | tf_op jit(solution)/shard_map/htqbk,bkhd->tqhd/dot_general | solution.py:26
  233.8 0.2 copy.62
  234.0 62.8 %all_to_all.20 = bf16[8,1,128,10,128]{4,2,3,1,0:T(8,128)(2,1)S(1)} all-to-all(bf16[8,1,128,10,128]{4,2,3,1,0:T(8,128)(2,1)S(1)} %copy.62), channel_id=1, replica_groups=mesh['head'=4,'st'=8] {'st'}, dimensions={0} | all-to-all | bytes 5242880 | tf_op jit(solution)/shard_map/all_to_all | solution.py:76
  296.8 0.3 copy.63
  297.1 3.2 %copy.64 = bf16[1,256,40,128]{3,2,1,0:T(8,128)(2,1)} copy(bf16[1,256,40,128]{3,1,2,0:T(8,128)(2,1)S(1)} %bitcast.57) | data formatting | bytes 5242880 | tf_op jit(solution)/shard_map/reshape | solution.py:79
  (1 shorter events, 0.0 us)
Async XLA Ops:
  4.2 66.8 %all-to-all-start = ((bf16[8,1,128,10,128]{4,2,3,1,0:T(8,128)(2,1)}), bf16[8,1,128,10,128]{4,2,3,1,0:T(8,128)(2,1)S(1)}, u32[]{:S(2)}, u32[]{:S(2)}) async-start(bf16[8,1,128,10,128]{4,2,3,1,0:T(8,128)(2,1)} %bitcast.55), calls=%async_computation | async-start | bytes 5242880 | tf_op jit(solution)/shard_map/all_to_all | solution.py:56
  13.8 61.6 %copy-start = (s32[8,10,8]{1,2,0:T(8,128)S(1)}, s32[8,10,8]{1,2,0:T(8,128)}, u32[]{:S(2)}) copy-start(s32[8,10,8]{1,2,0:T(8,128)} %param.7) | copy-start | bytes 7684
  71.0 83.8 %all-to-all-start.1 = ((bf16[8,1,128,10,128]{4,2,3,1,0:T(8,128)(2,1)}), bf16[8,1,128,10,128]{4,2,3,1,0:T(8,128)(2,1)}, u32[]{:S(2)}, u32[]{:S(2)}) async-start(bf16[8,1,128,10,128]{4,2,3,1,0:T(8,128)(2,1)} %bitcast.53), calls=%async_computation.1 | async-start | bytes 5242880 | tf_op jit(solution)/shard_map/all_to_all | solution.py:57
  154.8 59.3 %all-to-all-start.2 = ((bf16[8,1,128,10,128]{4,2,3,1,0:T(8,128)(2,1)}), bf16[8,1,128,10,128]{4,2,3,1,0:T(8,128)(2,1)}, u32[]{:S(2)}, u32[]{:S(2)}) async-start(bf16[8,1,128,10,128]{4,2,3,1,0:T(8,128)(2,1)} %bitcast.54), calls=%async_computation.2 | async-start | bytes 5242880 | tf_op jit(solution)/shard_map/all_to_all | solution.py:58
where the time goes:
time: 301 us; the launch traced here: 300 us
  blocking collectives  138 us (46%)
  waiting for transfers between devices  75.7 us (25%)
  matrix products  36.2 us (12%)
  other arithmetic  17.9 us (6%)
  local copies, waits for them, and re-layouts  16.6 us (6%)
  starting transfers between devices  16.1 us (5%)
    all_gather x1, blocking collectives, body(): lists_all = lax.all_gather(lists_heads, 'st', axis=0, tiled=True)  69.4 us
    all_to_all x1, blocking collectives, body(): lax.all_to_all(result, 'st', split_axis=0, concat_axis=0, tiled=True)  62.8 us
    all_to_all x1, waiting for transfers between devices, body(): lax.all_to_all(to_column(queries), 'st', split_axis=0, concat_axis=0, til...  55.3 us
    all_to_all x1, waiting for transfers between devices, body(): lax.all_to_all(to_column(value_vectors), 'st', split_axis=0, concat_axis=...  20.4 us
    dot_general x1, matrix products, attend_dense(): jnp.einsum('htqbk,bkhd->tqhd', weights.astype(jnp.bfloat16), value_blocks...  19.7 us
    reduce_sum x1, other arithmetic, attend_dense(): row_total = jnp.sum(weights, axis=(3, 4))  17.9 us
    dot_general x1, matrix products, attend_dense(): jnp.einsum('tqhd,bkhd->htqbk', query_tiles, key_blocks, preferred_element...  16.5 us
    all_to_all x1, starting transfers between devices, body(): lax.all_to_all(to_column(queries), 'st', split_axis=0, concat_axis=0, til...  7.28 us
  transfers between devices with their start and end apart: 3, of which 2 were waited for; matrix products, arithmetic and copies ran while one was open for 14% of the time, Pallas kernels for 0%

commit v1 on v0

v1 whole, which is shorter than its diff:
```python
import functools

import jax
import jax.numpy as jnp
from jax import lax
from jax.experimental import pallas as pl
from jax.experimental.pallas import tpu as pltpu
from jax.sharding import PartitionSpec as P

BLK = 128


def pack_kernel(q_ref, k_ref, v_ref, out_ref):
    owners, _, held, rows, width = out_ref.shape
    for slot, ref in enumerate((q_ref, k_ref, v_ref)):
        turned = pltpu.einshape("phd->hpd", ref[...])
        out_ref[:, slot] = turned.reshape(owners, held, rows, width)


def pack(queries, key_vectors, value_vectors, first, tubes, rows, devs):
    heads, width = queries.shape[1:]
    held = tubes * heads // devs
    owners = heads // held
    step = min(rows, 32)
    steps = rows // step
    source = pl.BlockSpec((step, heads, width), lambda t, i: ((first + t) * steps + i, 0, 0))
    return pl.pallas_call(
        pack_kernel,
        out_shape=jax.ShapeDtypeStruct((devs, 3, held, rows, width), queries.dtype),
        grid=(tubes, steps),
        in_specs=[source, source, source],
        out_specs=pl.BlockSpec((owners, 3, held, step, width), lambda t, i: (t, 0, 0, i, 0)),
        cost_estimate=pl.CostEstimate(
            flops=0, transcendentals=0, bytes_accessed=12 * devs * held * rows * width
        ),
        name="pack",
    )(queries, key_vectors, value_vectors)


def unpack_kernel(src_ref, *refs):
    out_ref = refs[-1]
    owners, held, rows, width = src_ref.shape
    out_ref[...] = pltpu.einshape("hpd->phd", src_ref[...].reshape(owners * held, rows, width))


def unpack(arrived, out, first, tubes, all_rows):
    devs, held, rows, width = arrived.shape
    owners = devs // tubes
    heads = owners * held
    step = min(rows, 32)
    steps = rows // step
    operands, in_specs, aliases = [arrived], [], {}
    in_specs.append(pl.BlockSpec((owners, held, step, width), lambda t, i: (t, 0, i, 0)))
    if out is not None:
        operands.append(out)
        in_specs.append(pl.BlockSpec(memory_space=pl.ANY))
        aliases = {1: 0}
    return pl.pallas_call(
        unpack_kernel,
        out_shape=jax.ShapeDtypeStruct((all_rows, heads, width), arrived.dtype),
        grid=(tubes, steps),
        in_specs=in_specs,
        out_specs=pl.BlockSpec(
            (step, heads, width), lambda t, i: ((first + t) * steps + i, 0, 0)
        ),
        input_output_aliases=aliases,
        cost_estimate=pl.CostEstimate(
            flops=0, transcendentals=0, bytes_accessed=4 * devs * held * rows * width
        ),
        name="unpack",
    )(*operands)


def attend_kernel(tiles, per_group, base_ref, lists_ref, q_ref, k_ref, v_ref, o_ref):
    frames, rows, width = q_ref.shape
    tokens = frames * rows
    span = BLK // rows
    group = 2
    entries = tokens // BLK
    head = base_ref[1] + pl.program_id(0)
    stride = per_group * entries
    start = base_ref[0] + (head // per_group) * (tiles * stride) + (head % per_group) * entries
    keys = k_ref[...].reshape(tokens, width)
    values = v_ref[...].reshape(tokens, width)
    block_of = lax.broadcasted_iota(jnp.int32, (1, tokens), 1) // BLK
    scale = width ** (-0.5)
    for pair in range(tiles // group):
        query = q_ref[pair * group * span : (pair + 1) * group * span]
        query = query.reshape(group * BLK, width)
        scores = lax.dot_general(
            query, keys, (((1,), (1,)), ((), ())), preferred_element_type=jnp.float32
        )
        parts = []
        for member in range(group):
            tile = pair * group + member
            bits = jnp.int32(0)
            for e in range(entries):
                block = lists_ref[start + tile * stride + e]
                bits = bits | jnp.where(block >= 0, 1 << jnp.maximum(block, 0), 0)
            chosen = ((bits >> block_of) & 1) == 1
            bias = jnp.where(chosen, 0.0, -jnp.inf)
            part = scores[member * BLK : (member + 1) * BLK] * scale + bias
            weights = jnp.exp(part - jnp.max(part, axis=1, keepdims=True))
            total = jnp.sum(weights, axis=1, keepdims=True)
            parts.append((weights.astype(jnp.bfloat16), total))
        rounded = jnp.concatenate([part for part, _ in parts], axis=0)
        totals = jnp.concatenate([total for _, total in parts], axis=0)
        summed = jnp.dot(rounded, values, preferred_element_type=jnp.float32)
        result = (summed / totals).astype(o_ref.dtype)
        o_ref[pair * group * span : (pair + 1) * group * span] = result.reshape(
            group * span, rows, width
        )


def attend(arrived, base, lists, tiles, per_group):
    devs, _, held, rows, width = arrived.shape
    tokens = devs * rows

    def part(slot):
        return pl.BlockSpec((devs, None, None, rows, width), lambda u, *_: (0, slot, u, 0, 0))

    return pl.pallas_call(
        functools.partial(attend_kernel, tiles, per_group),
        out_shape=jax.ShapeDtypeStruct((devs, held, rows, width), arrived.dtype),
        grid_spec=pltpu.PrefetchScalarGridSpec(
            num_scalar_prefetch=2,
            grid=(held,),
            in_specs=[part(0), part(1), part(2)],
            out_specs=pl.BlockSpec((devs, None, rows, width), lambda u, *_: (0, u, 0, 0)),
        ),
        cost_estimate=pl.CostEstimate(
            flops=4 * held * tokens * tokens * width,
            transcendentals=held * tokens * tokens,
            bytes_accessed=8 * held * tokens * width,
        ),
        name="attend",
    )(base, lists, arrived, arrived, arrived)


def exchange(blocks):
    return lax.all_to_all(blocks, "st", split_axis=0, concat_axis=0, tiled=True)


def body(queries, key_vectors, value_vectors, block_lists):
    head_devs = lax.axis_size("head")
    st_devs = lax.axis_size("st")
    local_frames, local_space, heads, width = queries.shape
    plane_tubes = st_devs // head_devs
    rows = local_frames * local_space // plane_tubes
    tiles, per_group, entries = block_lists.shape
    all_rows = local_frames * local_space
    chunk_tubes = 1 if heads % st_devs == 0 else plane_tubes
    held = chunk_tubes * heads // st_devs
    owners = heads // held

    def flat(source):
        shaped = source.reshape(local_frames, plane_tubes, -1, heads, width)
        return jnp.swapaxes(shaped, 0, 1).reshape(all_rows, heads, width)

    q_rows, k_rows, v_rows = flat(queries), flat(key_vectors), flat(value_vectors)
    head_at, st_at = lax.axis_index("head"), lax.axis_index("st")
    lists_all = lax.all_gather(block_lists.reshape(-1), ("st", "head"), axis=0, tiled=True)
    tube_size = tiles * heads * entries
    lists = lax.dynamic_slice(
        lists_all, (head_at * plane_tubes * tube_size,), (plane_tubes * tube_size,)
    )
    out = None
    for first in range(0, plane_tubes, chunk_tubes):
        arrived = exchange(pack(q_rows, k_rows, v_rows, first, chunk_tubes, rows, st_devs))
        base = jnp.stack([(first + st_at // owners) * tube_size, (st_at % owners) * held])
        result = attend(arrived, base, lists, tiles, per_group)
        out = unpack(exchange(result), out, first, chunk_tubes, all_rows)
    shaped = out.reshape(plane_tubes, local_frames, -1, heads, width)
    return jnp.swapaxes(shaped, 0, 1).reshape(queries.shape)


def solution(mesh):
    spec = P("st", "head", None, None)
    return jax.shard_map(
        body,
        mesh=mesh,
        in_specs=(spec, spec, spec, P("st", "head", None)),
        out_specs=spec,
        check_vma=False,
    )
```

time: 301 us -> 307 us (1.020)
  waiting for transfers between devices: 75.7 us -> 128 us
  Pallas kernels: 0 us -> 44.1 us
  blocking collectives: 138 us -> 98.5 us
  matrix products: 36.2 us -> 0 us
  other arithmetic: 17.9 us -> 1.31 us
  starting transfers between devices: 16.1 us -> 32.1 us
  local copies, waits for them, and re-layouts: 16.6 us -> 1.92 us
    all_to_all x1 -> x0, blocking collectives: 62.8 us -> none  [body(): lax.all_to_all(result, 'st', split_axis=0, concat_axis=0, tiled=True)]
    all_to_all x3 -> x4, waiting for transfers between devices: 75.7 us -> 128 us  [exchange(): return lax.all_to_all(blocks, 'st', split_axis=0, concat_axis=0, tiled=True)]
    pallas_call x0 -> x6, Pallas kernels: none -> 44.1 us  [the longest x2 27.5 us: attend(): pl.pallas_call(functools.partial(attend_kernel, tiles, per_group), out_sh...]
    dot_general x2 -> x0, matrix products: 36.2 us -> none  [the longest x1 19.7 us: attend_dense(): jnp.einsum('htqbk,bkhd->tqhd', weights.astype(jnp.bfloat16), value_blocks...]
    all_gather x2 -> x1, blocking collectives: 74.9 us -> 98.5 us  [body(): lax.all_gather(block_lists.reshape(-1), ('st', 'head'), axis=0, tiled=True)]
    reduce_sum x1 -> x0, other arithmetic: 17.9 us -> none  [attend_dense(): row_total = jnp.sum(weights, axis=(3, 4))]
    all_to_all x3 -> x4, starting transfers between devices: 16.1 us -> 32.1 us  [exchange(): return lax.all_to_all(blocks, 'st', split_axis=0, concat_axis=0, tiled=True)]
    unnamed x6 -> x8, local copies, waits for them, and re-layouts: 7.2 us -> 1.32 us
  transfers between devices with their start and end apart: 3 -> 4, of which waited for: 2 -> 3; matrix products, arithmetic and copies ran while one was open for 14% -> 1% of each run, Pallas kernels for 0% -> 12%
where the time goes in v1:
time: 307 us; the launch traced here: 306 us
  waiting for transfers between devices  128 us (42%)
  blocking collectives  98.5 us (32%)
  Pallas kernels  44.1 us (14%)
  starting transfers between devices  32.1 us (10%)
    all_to_all x4, waiting for transfers between devices, exchange(): return lax.all_to_all(blocks, 'st', split_axis=0, concat_axis=0, tiled=True)  128 us
    all_gather x1, blocking collectives, body(): lax.all_gather(block_lists.reshape(-1), ('st', 'head'), axis=0, tiled=True)  98.5 us
    all_to_all x4, starting transfers between devices, exchange(): return lax.all_to_all(blocks, 'st', split_axis=0, concat_axis=0, tiled=True)  32.1 us
    pallas_call x2, Pallas kernels, attend(): pl.pallas_call(functools.partial(attend_kernel, tiles, per_group), out_sh...  27.5 us
    pallas_call x2, Pallas kernels, pack(): pl.pallas_call(pack_kernel, out_shape=jax.ShapeDtypeStruct((devs, 3, held...  9.51 us
    pallas_call x2, Pallas kernels, unpack(): pl.pallas_call(unpack_kernel, out_shape=jax.ShapeDtypeStruct((all_rows, h...  7 us
  transfers between devices with their start and end apart: 4, of which 3 were waited for; matrix products, arithmetic and copies ran while one was open for 1% of the time, Pallas kernels for 12%

profile of v1, /device:TPU:0, one launch (start us, length us, event | category | flops | bytes accessed | tf_op | source)
XLA Modules:
  0.0 306.3 jit_solution(10063015997729567219)
XLA Ops:
  0.0 4.7 %pack.3 = bf16[8,3,5,128,128]{4,3,2,1,0:T(8,128)(2,1)} custom-call(bf16[256,40,128]{2,1,0:T(8,128)(2,1)} %bitcast.8, bf16[256,40,128]{2,1,0:T(8,128)(2,1)} %bitcast.10, bf16[256,40,128]{2,1,0:T(8,128)(2,1)} %bitcast.12), custom_call_target="tpu_custom_call" | custom-call | bytes 7864320 | tf_op jit(solution)/shard_map/pack/pallas_call | solution.py:27
  4.7 7.3 %all-to-all-start.2 = ((bf16[8,3,5,128,128]{4,3,2,1,0:T(8,128)(2,1)}), bf16[8,3,5,128,128]{4,3,2,1,0:T(8,128)(2,1)}, u32[]{:S(2)}, u32[]{:S(2)}) async-start(bf16[8,3,5,128,128]{4,3,2,1,0:T(8,128)(2,1)} %pack.3), calls=%async_computation.2 | async-start | bytes 7864320 | tf_op jit(solution)/shard_map/all_to_all | solution.py:141
  12.0 4.8 %pack.2 = bf16[8,3,5,128,128]{4,3,2,1,0:T(8,128)(2,1)} custom-call(bf16[256,40,128]{2,1,0:T(8,128)(2,1)} %bitcast.9, bf16[256,40,128]{2,1,0:T(8,128)(2,1)} %bitcast.11, bf16[256,40,128]{2,1,0:T(8,128)(2,1)} %bitcast.13), custom_call_target="tpu_custom_call" | custom-call | bytes 7864320 | tf_op jit(solution)/shard_map/pack/pallas_call | solution.py:27
  16.8 0.0 copy-start.2
  16.8 82.9 %all-to-all-done.2.q_ref.k_ref.v_ref = bf16[8,3,5,128,128]{4,3,2,1,0:T(8,128)(2,1)} async-done(((bf16[8,3,5,128,128]{4,3,2,1,0:T(8,128)(2,1)}), bf16[8,3,5,128,128]{4,3,2,1,0:T(8,128)(2,1)}, u32[]{:S(2)}, u32[]{:S(2)}) %all-to-all-start.2) | async-done | bytes 3932192 | tf_op jit(solution)/shard_map/all_to_all | solution.py:141
  99.7 4.5 %all-to-all-start = ((bf16[8,3,5,128,128]{4,3,2,1,0:T(8,128)(2,1)}), bf16[8,3,5,128,128]{4,3,2,1,0:T(8,128)(2,1)}, u32[]{:S(2)}, u32[]{:S(2)}) async-start(bf16[8,3,5,128,128]{4,3,2,1,0:T(8,128)(2,1)} %pack.2), calls=%async_computation | async-start | bytes 7864320 | tf_op jit(solution)/shard_map/all_to_all | solution.py:141
  104.2 0.0 copy-done.2
  104.3 0.1 copy.7
  104.4 0.1 reshape.4
  104.5 98.5 %all-gather = s32[32,1,640]{2,1,0:T(1,128)S(1)} all-gather(s32[1,1,640]{2,1,0:T(1,128)S(1)} %reshape.4), channel_id=1, replica_groups=mesh['head'=4,'st'=8] {'st','head'}, dimensions={0}, use_global_device_ids=true | all-gather | bytes 84480 | tf_op jit(solution)/shard_map/all_gather | solution.py:162
  202.9 0.6 dynamic_slice.3.lists_ref
  203.5 0.7 pad_add_fusion.1.base_ref
  204.2 13.8 %attend.3 = bf16[8,5,128,128]{3,2,1,0:T(8,128)(2,1)} custom-call(s32[2]{0:T(128)} %pad_add_fusion.1.base_ref, s32[5120]{0:T(1024)} %dynamic_slice.3.lists_ref, bf16[8,3,5,128,128]{4,3,2,1,0:T(8,128)(2,1)} %all-to-all-done.2.q_ref.k_ref.v_ref, bf16[8,3,5,128,128]{4,3,2,1,0:T(8,128)(2,1)} %all-to-all-done.2.q_ref.k_ref.v_ref, ...), custom_call_target="tpu_custom_call" | custom-call | flops 2684354560 | bytes 5242880 | tf_op jit(solution)/shard_map/attend/pallas_call | solution.py:122
  218.0 0.0 all-to-all-done.q_ref.k_ref.v_ref
  218.0 16.6 %all-to-all-start.3 = ((bf16[8,5,128,128]{3,2,1,0:T(8,128)(2,1)}), bf16[8,5,128,128]{3,2,1,0:T(8,128)(2,1)S(1)}, u32[]{:S(2)}, u32[]{:S(2)}) async-start(bf16[8,5,128,128]{3,2,1,0:T(8,128)(2,1)} %attend.3), calls=%async_computation.3 | async-start | bytes 2621440 | tf_op jit(solution)/shard_map/all_to_all | solution.py:141
  234.6 0.6 pad_add_fusion.base_ref
  235.2 13.8 %attend.2 = bf16[8,5,128,128]{3,2,1,0:T(8,128)(2,1)} custom-call(s32[2]{0:T(128)} %pad_add_fusion.base_ref, s32[5120]{0:T(1024)} %dynamic_slice.3.lists_ref, bf16[8,3,5,128,128]{4,3,2,1,0:T(8,128)(2,1)} %all-to-all-done.q_ref.k_ref.v_ref, bf16[8,3,5,128,128]{4,3,2,1,0:T(8,128)(2,1)} %all-to-all-done.q_ref.k_ref.v_ref, ...), custom_call_target="tpu_custom_call" | custom-call | flops 2684354560 | bytes 5242880 | tf_op jit(solution)/shard_map/attend/pallas_call | solution.py:122
  249.0 17.4 %all-to-all-done.3.src_ref = bf16[8,5,128,128]{3,2,1,0:T(8,128)(2,1)S(1)} async-done(((bf16[8,5,128,128]{3,2,1,0:T(8,128)(2,1)}), bf16[8,5,128,128]{3,2,1,0:T(8,128)(2,1)S(1)}, u32[]{:S(2)}, u32[]{:S(2)}) %all-to-all-start.3) | async-done | bytes 1310752 | tf_op jit(solution)/shard_map/all_to_all | solution.py:141
  266.5 0.0 copy-start
  266.5 3.6 %all-to-all-start.1 = ((bf16[8,5,128,128]{3,2,1,0:T(8,128)(2,1)}), bf16[8,5,128,128]{3,2,1,0:T(8,128)(2,1)S(1)}, u32[]{:S(2)}, u32[]{:S(2)}) async-start(bf16[8,5,128,128]{3,2,1,0:T(8,128)(2,1)} %attend.2), calls=%async_computation.1 | async-start | bytes 2621440 | tf_op jit(solution)/shard_map/all_to_all | solution.py:141
  270.1 0.0 copy-done
  270.1 3.5 %unpack.2.refs_0_ = bf16[256,40,128]{2,1,0:T(8,128)(2,1)} custom-call(bf16[8,5,128,128]{3,2,1,0:T(8,128)(2,1)} %copy-done), custom_call_target="tpu_custom_call" | custom-call | bytes 2621440 | tf_op jit(solution)/shard_map/unpack/pallas_call | solution.py:58
  273.6 28.1 %all-to-all-done.1.src_ref = bf16[8,5,128,128]{3,2,1,0:T(8,128)(2,1)S(1)} async-done(((bf16[8,5,128,128]{3,2,1,0:T(8,128)(2,1)}), bf16[8,5,128,128]{3,2,1,0:T(8,128)(2,1)S(1)}, u32[]{:S(2)}, u32[]{:S(2)}) %all-to-all-start.1) | async-done | bytes 1310752 | tf_op jit(solution)/shard_map/all_to_all | solution.py:141
  301.7 0.0 copy-start.1
  301.7 1.1 copy-done.1
  302.8 3.5 %unpack.3 = bf16[256,40,128]{2,1,0:T(8,128)(2,1)} custom-call(bf16[8,5,128,128]{3,2,1,0:T(8,128)(2,1)} %copy-done.1, bf16[256,40,128]{2,1,0:T(8,128)(2,1)} %unpack.2.refs_0_), custom_call_target="tpu_custom_call", output_to_operand_aliasing={{}: (1, {})} | custom-call | bytes 2621440 | tf_op jit(solution)/shard_map/unpack/pallas_call | solution.py:58
Async XLA Ops:
  4.7 94.9 %all-to-all-start.2 = ((bf16[8,3,5,128,128]{4,3,2,1,0:T(8,128)(2,1)}), bf16[8,3,5,128,128]{4,3,2,1,0:T(8,128)(2,1)}, u32[]{:S(2)}, u32[]{:S(2)}) async-start(bf16[8,3,5,128,128]{4,3,2,1,0:T(8,128)(2,1)} %pack.3), calls=%async_computation.2 | async-start | bytes 7864320 | tf_op jit(solution)/shard_map/all_to_all | solution.py:141
  16.8 87.5 %copy-start.2 = (s32[8,10,8]{1,2,0:T(8,128)S(1)}, s32[8,10,8]{1,2,0:T(8,128)}, u32[]{:S(2)}) copy-start(s32[8,10,8]{1,2,0:T(8,128)} %param.7) | copy-start | bytes 7684
  99.7 118.3 %all-to-all-start = ((bf16[8,3,5,128,128]{4,3,2,1,0:T(8,128)(2,1)}), bf16[8,3,5,128,128]{4,3,2,1,0:T(8,128)(2,1)}, u32[]{:S(2)}, u32[]{:S(2)}) async-start(bf16[8,3,5,128,128]{4,3,2,1,0:T(8,128)(2,1)} %pack.2), calls=%async_computation | async-start | bytes 7864320 | tf_op jit(solution)/shard_map/all_to_all | solution.py:141
  218.0 48.5 %all-to-all-start.3 = ((bf16[8,5,128,128]{3,2,1,0:T(8,128)(2,1)}), bf16[8,5,128,128]{3,2,1,0:T(8,128)(2,1)S(1)}, u32[]{:S(2)}, u32[]{:S(2)}) async-start(bf16[8,5,128,128]{3,2,1,0:T(8,128)(2,1)} %attend.3), calls=%async_computation.3 | async-start | bytes 2621440 | tf_op jit(solution)/shard_map/all_to_all | solution.py:141
  266.5 3.6 %copy-start = (bf16[8,5,128,128]{3,2,1,0:T(8,128)(2,1)}, bf16[8,5,128,128]{3,2,1,0:T(8,128)(2,1)S(1)}, u32[]{:S(2)}) copy-start(bf16[8,5,128,128]{3,2,1,0:T(8,128)(2,1)S(1)} %all-to-all-done.3.src_ref) | copy-start | bytes 3932164
  266.5 35.2 %all-to-all-start.1 = ((bf16[8,5,128,128]{3,2,1,0:T(8,128)(2,1)}), bf16[8,5,128,128]{3,2,1,0:T(8,128)(2,1)S(1)}, u32[]{:S(2)}, u32[]{:S(2)}) async-start(bf16[8,5,128,128]{3,2,1,0:T(8,128)(2,1)} %attend.2), calls=%async_computation.1 | async-start | bytes 2621440 | tf_op jit(solution)/shard_map/all_to_all | solution.py:141
  301.7 1.1 copy-start.1

commit v2 on v1

--- a/solution.py
+++ b/solution.py
@@ -137,6 +137,48 @@
     )(base, lists, arrived, arrived, arrived)
 
 
+def attend_own_kernel(q_ref, k_ref, v_ref, o_ref):
+    owners, _, width = q_ref.shape
+    scale = width ** (-0.5)
+    heads = range(owners)
+    scores = [
+        lax.dot_general(
+            q_ref[h], k_ref[h], (((1,), (1,)), ((), ())), preferred_element_type=jnp.float32
+        )
+        for h in heads
+    ]
+    weights, totals = [], []
+    for h in heads:
+        part = scores[h] * scale
+        part = jnp.exp(part - jnp.max(part, axis=1, keepdims=True))
+        totals.append(jnp.sum(part, axis=1, keepdims=True))
+        weights.append(part.astype(jnp.bfloat16))
+    for h in heads:
+        summed = jnp.dot(weights[h], v_ref[h], preferred_element_type=jnp.float32)
+        o_ref[h] = (summed / totals[h]).astype(o_ref.dtype)
+
+
+def attend_own(packed):
+    owners, _, held, rows, width = packed.shape
+
+    def part(slot):
+        return pl.BlockSpec((owners, None, None, rows, width), lambda u: (0, slot, u, 0, 0))
+
+    return pl.pallas_call(
+        attend_own_kernel,
+        out_shape=jax.ShapeDtypeStruct((owners, held, rows, width), packed.dtype),
+        grid=(held,),
+        in_specs=[part(0), part(1), part(2)],
+        out_specs=pl.BlockSpec((owners, None, rows, width), lambda u: (0, u, 0, 0)),
+        cost_estimate=pl.CostEstimate(
+            flops=4 * owners * held * rows * rows * width,
+            transcendentals=owners * held * rows * rows,
+            bytes_accessed=8 * owners * held * rows * width,
+        ),
+        name="attend_own",
+    )(packed, packed, packed)
+
+
 def exchange(blocks):
     return lax.all_to_all(blocks, "st", split_axis=0, concat_axis=0, tiled=True)
 
@@ -151,25 +193,60 @@
     all_rows = local_frames * local_space
     chunk_tubes = 1 if heads % st_devs == 0 else plane_tubes
     held = chunk_tubes * heads // st_devs
-    owners = heads // held
+    owners = st_devs // chunk_tubes
+    chunks = plane_tubes // chunk_tubes
 
     def flat(source):
         shaped = source.reshape(local_frames, plane_tubes, -1, heads, width)
         return jnp.swapaxes(shaped, 0, 1).reshape(all_rows, heads, width)
 
-    q_rows, k_rows, v_rows = flat(queries), flat(key_vectors), flat(value_vectors)
+    tensors = flat(queries), flat(key_vectors), flat(value_vectors)
     head_at, st_at = lax.axis_index("head"), lax.axis_index("st")
-    lists_all = lax.all_gather(block_lists.reshape(-1), ("st", "head"), axis=0, tiled=True)
     tube_size = tiles * heads * entries
-    lists = lax.dynamic_slice(
-        lists_all, (head_at * plane_tubes * tube_size,), (plane_tubes * tube_size,)
-    )
-    out = None
-    for first in range(0, plane_tubes, chunk_tubes):
-        arrived = exchange(pack(q_rows, k_rows, v_rows, first, chunk_tubes, rows, st_devs))
-        base = jnp.stack([(first + st_at // owners) * tube_size, (st_at % owners) * held])
-        result = attend(arrived, base, lists, tiles, per_group)
-        out = unpack(exchange(result), out, first, chunk_tubes, all_rows)
+    mine = block_lists.reshape(-1, 128 if block_lists.size % 128 == 0 else entries)
+    mine = lax.all_gather(mine, "head", axis=0, tiled=True)
+    every = exchange(jnp.broadcast_to(mine, (st_devs, *mine.shape)))
+    lists = lax.dynamic_slice_in_dim(every, head_at * plane_tubes, plane_tubes, 0)
+    packed = [
+        pack(*tensors, c * chunk_tubes, chunk_tubes, rows, st_devs) for c in range(chunks)
+    ]
+
+    def run(travels, packed, lists):
+        out, arrived = None, {}
+        for c in range(chunks):
+            if travels[c]:
+                arrived[c] = exchange(packed[c])
+        for c in range(chunks):
+            if not travels[c]:
+                result = attend_own(packed[c])
+                out = unpack(result, out, c * chunk_tubes, chunk_tubes, all_rows)
+        for c, blocks in arrived.items():
+            if out is not None and len(arrived) < chunks:
+                blocks, out = lax.optimization_barrier((blocks, out))
+            base = jnp.stack([(c + st_at // owners) * tube_size, (st_at % owners) * held])
+            result = attend(blocks, base, lists, tiles, per_group)
+            result = exchange(result)
+            arrived[c] = result
+        for c, result in arrived.items():
+            out = unpack(result, out, c * chunk_tubes, chunk_tubes, all_rows)
+        return out
+
+    if rows == BLK and tiles == st_devs and chunk_tubes == 1 and plane_tubes <= 2:
+        place = jnp.arange(tube_size) % (per_group * tiles * entries)
+        tile_of = (place // (per_group * entries)).reshape(lists.shape[1:])[None]
+        own = jnp.all((lists == tile_of) | (lists == -1), axis=(1, 2))
+        which = jnp.sum(jnp.where(own, 0, 1 << jnp.arange(plane_tubes)))
+
+        def branch(code):
+            def go(packed, lists):
+                return run([bool((code >> c) & 1) for c in range(chunks)], packed, lists)
+
+            return go
+
+        branches = [branch(code) for code in range(1 << chunks)]
+        out = lax.switch(which, branches, packed, lists.reshape(-1))
+    else:
+        out = run([True] * chunks, packed, lists.reshape(-1))
     shaped = out.reshape(plane_tubes, local_frames, -1, heads, width)
     return jnp.swapaxes(shaped, 0, 1).reshape(queries.shape)
 

time: 307 us -> 229 us (0.75)
  the two profiles are of different devices: /device:TPU:0 before, /device:TPU:5 now
where the time goes in v2:
time: 229 us; the launch traced here: 228 us
  blocking collectives  98 us (43%)
  waiting for transfers between devices  63 us (28%)
  Pallas kernels  43.7 us (19%)
  starting transfers between devices  17.4 us (8%)
  local copies, waits for them, and re-layouts  2.78 us (1%)
    all_to_all x1, blocking collectives, exchange(): return lax.all_to_all(blocks, 'st', split_axis=0, concat_axis=0, tiled=True)  92.3 us
    all_to_all x4, waiting for transfers between devices, exchange(): return lax.all_to_all(blocks, 'st', split_axis=0, concat_axis=0, tiled=True)  63 us
    pallas_call x2, Pallas kernels, attend(): pl.pallas_call(functools.partial(attend_kernel, tiles, per_group), out_sh...  27.3 us
    all_to_all x4, starting transfers between devices, exchange(): return lax.all_to_all(blocks, 'st', split_axis=0, concat_axis=0, tiled=True)  17.4 us
    pallas_call x2, Pallas kernels, pack(): pl.pallas_call(pack_kernel, out_shape=jax.ShapeDtypeStruct((devs, 3, held...  9.47 us
    pallas_call x2, Pallas kernels, unpack(): pl.pallas_call(unpack_kernel, out_shape=jax.ShapeDtypeStruct((all_rows, h...  7 us
    all_gather x1, blocking collectives, body(): mine = lax.all_gather(mine, 'head', axis=0, tiled=True)  5.71 us
  transfers between devices with their start and end apart: 4, of which 3 were waited for; matrix products, arithmetic and copies ran while one was open for 1% of the time, Pallas kernels for 18%

profile of v2, /device:TPU:5, one launch (start us, length us, event | category | flops | bytes accessed | tf_op | source)
XLA Modules:
  0.0 227.7 jit_solution(15014371367440483054)
XLA Ops:
  0.0 0.9 copy.14
  0.9 0.1 reshape.29
  1.0 5.7 %all-gather = s32[4,5,128]{2,1,0:T(8,128)S(1)} all-gather(s32[1,5,128]{2,1,0:T(8,128)S(1)} %reshape.29), channel_id=1, replica_groups=mesh['head'=4,'st'=8] {'head'}, dimensions={0}, use_global_device_ids=true | all-gather | bytes 12800 | tf_op jit(solution)/shard_map/all_gather | solution.py:207
  6.7 0.7 broadcast_in_dim.7
  7.3 5.5 %all-to-all-start.8 = ((s32[8,20,128]{2,1,0:T(8,128)}), s32[8,20,128]{2,1,0:T(8,128)S(1)}, u32[]{:S(2)}, u32[]{:S(2)}) async-start(s32[8,20,128]{2,1,0:T(8,128)} %broadcast_in_dim.7), calls=%async_computation.8 | async-start | bytes 196608 | tf_op jit(solution)/shard_map/all_to_all | solution.py:183
  12.9 4.8 %pack.3 = bf16[8,3,5,128,128]{4,3,2,1,0:T(8,128)(2,1)} custom-call(bf16[256,40,128]{2,1,0:T(8,128)(2,1)} %bitcast.14, bf16[256,40,128]{2,1,0:T(8,128)(2,1)} %bitcast.16, bf16[256,40,128]{2,1,0:T(8,128)(2,1)} %bitcast.18), custom_call_target="tpu_custom_call" | custom-call | bytes 7864320 | tf_op jit(solution)/shard_map/pack/pallas_call | solution.py:27
  17.6 4.7 %pack.2 = bf16[8,3,5,128,128]{4,3,2,1,0:T(8,128)(2,1)} custom-call(bf16[256,40,128]{2,1,0:T(8,128)(2,1)} %bitcast.15, bf16[256,40,128]{2,1,0:T(8,128)(2,1)} %bitcast.17, bf16[256,40,128]{2,1,0:T(8,128)(2,1)} %bitcast.19), custom_call_target="tpu_custom_call" | custom-call | bytes 7864320 | tf_op jit(solution)/shard_map/pack/pallas_call | solution.py:27
  22.4 0.0 all-to-all-done.8
  22.4 0.1 or_reduce_fusion
  22.5 0.6 select_reduce_fusion
  23.8 203.9 %conditional.1 = (bf16[1,256,40,128]{3,2,1,0:T(8,128)(2,1)}) conditional(s32[]{:T(128)} %clamp.3, (bf16[8,3,5,128,128]{4,3,2,1,0:T(8,128)(2,1)}, bf16[8,3,5,128,128]{4,3,2,1,0:T(8,128)(2,1)}) %tuple.23, (s32[]{:T(128)}, bf16[8,3,5,128,128]{4,3,2,1,0:T(8,128)(2,1)}, bf16[8,3,5,128,128]{4,3,2,1,0:T(8,128)(2,1)}, ...), branch_computations={%region_2.3_spmd, %region_3.4_spmd, %region_4.5_spmd, %region_5.6_... | conditional | flops 5368709120 | bytes 53739948 | solution.py:247
  23.8 92.3 %all_to_all.39.q_ref.k_ref.v_ref = bf16[8,3,5,128,128]{4,3,2,1,0:T(8,128)(2,1)} all-to-all(bf16[8,3,5,128,128]{4,3,2,1,0:T(8,128)(2,1)} %get-tuple-element.56), channel_id=1, replica_groups=mesh['head'=4,'st'=8] {'st'}, dimensions={0} | all-to-all | bytes 7864320 | tf_op jit(solution)/shard_map/cond/branch_3_fun/all_to_all | solution.py:183
  116.2 4.6 %all-to-all-start.4 = ((bf16[8,3,5,128,128]{4,3,2,1,0:T(8,128)(2,1)}), bf16[8,3,5,128,128]{4,3,2,1,0:T(8,128)(2,1)}, u32[]{:S(2)}, u32[]{:S(2)}) async-start(bf16[8,3,5,128,128]{4,3,2,1,0:T(8,128)(2,1)} %get-tuple-element.55), calls=%async_computation.4 | async-start | bytes 7864320 | tf_op jit(solution)/shard_map/cond/branch_3_fun/all_to_all | solution.py:183
  120.7 0.6 pad_add_fusion.3.base_ref
  121.3 13.6 %attend.7 = bf16[8,5,128,128]{3,2,1,0:T(8,128)(2,1)} custom-call(s32[2]{0:T(128)} %pad_add_fusion.3.base_ref, s32[5120]{0:T(1024)S(1)} %get-tuple-element.54.lists_ref, bf16[8,3,5,128,128]{4,3,2,1,0:T(8,128)(2,1)} %all_to_all.39.q_ref.k_ref.v_ref, bf16[8,3,5,128,128]{4,3,2,1,0:T(8,128)(2,1)} %all_to_all.39.q_ref.k_ref.v_ref, ...), custom_call_target="tpu_custom_call" | custom-call | flops 2684354560 | bytes 5242880 | tf_op jit(solution)/shard_map/cond/branch_3_fun/attend/pallas_call | solution.py:122
  134.9 45.8 %all-to-all-done.4.q_ref.k_ref.v_ref = bf16[8,3,5,128,128]{4,3,2,1,0:T(8,128)(2,1)} async-done(((bf16[8,3,5,128,128]{4,3,2,1,0:T(8,128)(2,1)}), bf16[8,3,5,128,128]{4,3,2,1,0:T(8,128)(2,1)}, u32[]{:S(2)}, u32[]{:S(2)}) %all-to-all-start.4) | async-done | bytes 3932192 | tf_op jit(solution)/shard_map/cond/branch_3_fun/all_to_all | solution.py:183
  180.7 3.8 %all-to-all-start.7 = ((bf16[8,5,128,128]{3,2,1,0:T(8,128)(2,1)}), bf16[8,5,128,128]{3,2,1,0:T(8,128)(2,1)S(1)}, u32[]{:S(2)}, u32[]{:S(2)}) async-start(bf16[8,5,128,128]{3,2,1,0:T(8,128)(2,1)} %attend.7), calls=%async_computation.7 | async-start | bytes 2621440 | tf_op jit(solution)/shard_map/cond/branch_3_fun/all_to_all | solution.py:183
  184.5 0.7 pad_add_fusion.2.base_ref
  185.1 13.7 %attend.6 = bf16[8,5,128,128]{3,2,1,0:T(8,128)(2,1)} custom-call(s32[2]{0:T(128)} %pad_add_fusion.2.base_ref, s32[5120]{0:T(1024)S(1)} %get-tuple-element.54.lists_ref, bf16[8,3,5,128,128]{4,3,2,1,0:T(8,128)(2,1)} %all-to-all-done.4.q_ref.k_ref.v_ref, bf16[8,3,5,128,128]{4,3,2,1,0:T(8,128)(2,1)} %all-to-all-done.4.q_ref.k_ref.v_ref, ...), custom_call_target="tpu_custom_call" | custom-call | flops 2684354560 | bytes 5242880 | tf_op jit(solution)/shard_map/cond/branch_3_fun/attend/pallas_call | solution.py:122
  198.8 3.0 %all-to-all-done.7.src_ref = bf16[8,5,128,128]{3,2,1,0:T(8,128)(2,1)S(1)} async-done(((bf16[8,5,128,128]{3,2,1,0:T(8,128)(2,1)}), bf16[8,5,128,128]{3,2,1,0:T(8,128)(2,1)S(1)}, u32[]{:S(2)}, u32[]{:S(2)}) %all-to-all-start.7) | async-done | bytes 1310752 | tf_op jit(solution)/shard_map/cond/branch_3_fun/all_to_all | solution.py:183
  201.8 0.0 copy-start
  201.8 3.6 %all-to-all-start.5 = ((bf16[8,5,128,128]{3,2,1,0:T(8,128)(2,1)}), bf16[8,5,128,128]{3,2,1,0:T(8,128)(2,1)S(1)}, u32[]{:S(2)}, u32[]{:S(2)}) async-start(bf16[8,5,128,128]{3,2,1,0:T(8,128)(2,1)} %attend.6), calls=%async_computation.5 | async-start | bytes 2621440 | tf_op jit(solution)/shard_map/cond/branch_3_fun/all_to_all | solution.py:183
  205.4 0.0 copy-done
  205.4 3.5 %unpack.14.refs_0_ = bf16[256,40,128]{2,1,0:T(8,128)(2,1)} custom-call(bf16[8,5,128,128]{3,2,1,0:T(8,128)(2,1)} %copy-done), custom_call_target="tpu_custom_call" | custom-call | bytes 2621440 | tf_op jit(solution)/shard_map/cond/branch_3_fun/unpack/pallas_call | solution.py:58
  208.9 14.2 %all-to-all-done.5.src_ref = bf16[8,5,128,128]{3,2,1,0:T(8,128)(2,1)S(1)} async-done(((bf16[8,5,128,128]{3,2,1,0:T(8,128)(2,1)}), bf16[8,5,128,128]{3,2,1,0:T(8,128)(2,1)S(1)}, u32[]{:S(2)}, u32[]{:S(2)}) %all-to-all-start.5) | async-done | bytes 1310752 | tf_op jit(solution)/shard_map/cond/branch_3_fun/all_to_all | solution.py:183
  223.1 0.0 copy-start.1
  223.1 1.2 copy-done.1
  224.2 3.5 %unpack.15 = bf16[256,40,128]{2,1,0:T(8,128)(2,1)} custom-call(bf16[8,5,128,128]{3,2,1,0:T(8,128)(2,1)} %copy-done.1, bf16[256,40,128]{2,1,0:T(8,128)(2,1)} %unpack.14.refs_0_), custom_call_target="tpu_custom_call", output_to_operand_aliasing={{}: (1, {})} | custom-call | bytes 2621440 | tf_op jit(solution)/shard_map/cond/branch_3_fun/unpack/pallas_call | solution.py:58
  (3 shorter events, 0.0 us)
Async XLA Ops:
  7.3 15.0 %all-to-all-start.8 = ((s32[8,20,128]{2,1,0:T(8,128)}), s32[8,20,128]{2,1,0:T(8,128)S(1)}, u32[]{:S(2)}, u32[]{:S(2)}) async-start(s32[8,20,128]{2,1,0:T(8,128)} %broadcast_in_dim.7), calls=%async_computation.8 | async-start | bytes 196608 | tf_op jit(solution)/shard_map/all_to_all | solution.py:183
  116.2 64.5 %all-to-all-start.4 = ((bf16[8,3,5,128,128]{4,3,2,1,0:T(8,128)(2,1)}), bf16[8,3,5,128,128]{4,3,2,1,0:T(8,128)(2,1)}, u32[]{:S(2)}, u32[]{:S(2)}) async-start(bf16[8,3,5,128,128]{4,3,2,1,0:T(8,128)(2,1)} %get-tuple-element.55), calls=%async_computation.4 | async-start | bytes 7864320 | tf_op jit(solution)/shard_map/cond/branch_3_fun/all_to_all | solution.py:183
  180.7 21.1 %all-to-all-start.7 = ((bf16[8,5,128,128]{3,2,1,0:T(8,128)(2,1)}), bf16[8,5,128,128]{3,2,1,0:T(8,128)(2,1)S(1)}, u32[]{:S(2)}, u32[]{:S(2)}) async-start(bf16[8,5,128,128]{3,2,1,0:T(8,128)(2,1)} %attend.7), calls=%async_computation.7 | async-start | bytes 2621440 | tf_op jit(solution)/shard_map/cond/branch_3_fun/all_to_all | solution.py:183
  201.8 3.6 %copy-start = (bf16[8,5,128,128]{3,2,1,0:T(8,128)(2,1)}, bf16[8,5,128,128]{3,2,1,0:T(8,128)(2,1)S(1)}, u32[]{:S(2)}) copy-start(bf16[8,5,128,128]{3,2,1,0:T(8,128)(2,1)S(1)} %all-to-all-done.7.src_ref) | copy-start | bytes 3932164 | tf_op jit(solution)/shard_map/cond
  201.8 21.3 %all-to-all-start.5 = ((bf16[8,5,128,128]{3,2,1,0:T(8,128)(2,1)}), bf16[8,5,128,128]{3,2,1,0:T(8,128)(2,1)S(1)}, u32[]{:S(2)}, u32[]{:S(2)}) async-start(bf16[8,5,128,128]{3,2,1,0:T(8,128)(2,1)} %attend.6), calls=%async_computation.5 | async-start | bytes 2621440 | tf_op jit(solution)/shard_map/cond/branch_3_fun/all_to_all | solution.py:183
  223.1 1.2 copy-start.1
